TPU v7x, 256 devices: a whole 4x4x8 slice. The times are simulated.
256 devices in a mesh: seq: 64 (over z_hi, y, x, core), tp: 4 (over z_lo).
Axes of the slice: x: 4, y: 4, z: 8 (z_hi: 2, z_lo: 4; z = z_hi * 4 + z_lo), core: 2. Of those that a mesh axis runs over, the one named last changes fastest.
Arguments:
- tokens: bfloat16 [8192, 2048], P(('seq', 'tp')), may hold values from -6 to 6
- block_ids: int32 [64, 2], replicated, may hold values from 0 to 127, as said below
- attn_gain: float32 [2048], replicated, may hold values from 0.25 to 1.75
- q_weight: bfloat16 [2048, 3072], P(None, 'tp'), may hold values from -0.125 to 0.125
- kv_weight: bfloat16 [2048, 576], replicated, may hold values from -0.125 to 0.125
- kv_gain: float32 [512], replicated, may hold values from 0.25 to 1.75
- uk_weight: bfloat16 [16, 512, 128], P('tp'), may hold values from -40 to 40
- uv_weight: bfloat16 [16, 512, 128], P('tp'), may hold values from -0.25 to 0.25
- o_weight: bfloat16 [2048, 2048], P('tp'), may hold values from -0.125 to 0.125
- ffn_gain: float32 [2048], replicated, may hold values from 0.25 to 1.75
- w_gate: bfloat16 [64, 2048, 1408], P('seq', None, 'tp'), may hold values from -0.125 to 0.125
- w_up: bfloat16 [64, 2048, 1408], P('seq', None, 'tp'), may hold values from -0.125 to 0.125
- w_down: bfloat16 [64, 1408, 2048], P('seq', 'tp'), may hold values from -0.15625 to 0.15625
- routes: int32 [8192, 6], P('seq'), may hold values from 0 to 63, all different within a row; in each aligned block of 32 rows (0 to 31, 32 to 63, ...) at most 4 rows name the same one
- gate_weights: float32 [8192, 6], P('seq'), may hold values from 0.1 to 1
Outputs:
- layer_out: bfloat16 [8192, 2048], P(('seq', 'tp'))
Inputs may be any that keep to these rules, and one draw needn't show every extreme that they name: `block_ids`: row d is (b, 127 - b) with b below 64; the first column names every b once. `routes`: each row names 6 different experts. In each aligned block of 32 rows (the tokens of one device) no expert is named by more than 4 rows, a bound that some block reaches.
All inputs are finite; a program needn't handle non-finite values.
Results may differ from a plain program's by a relative error of at most 0.027.
The roundings to bfloat16 on the way count: a program that leaves them out, or rounds other values in their place, can miss the bound.
Values may be sent and summed in bfloat16 or wider, within the bound.
A program may use at most 128 MiB of HBM per device.

v0:
```python
import math
import jax
import jax.numpy as jnp
from jax import lax
from jax.sharding import PartitionSpec as P

EPSILON = 1e-06


def normalize(values, gain_vec):
    values = values.astype(jnp.float32)
    factor = lax.rsqrt(jnp.mean(values * values, axis=-1, keepdims=True) + EPSILON)
    return values * factor * gain_vec


def rotate(values, position):
    half_width = values.shape[-1] // 2
    frequency = jnp.exp(
        jnp.arange(half_width, dtype=jnp.float32) * (-2.0 * math.log(10000.0) / values.shape[-1])
    )
    angles = (
        position.astype(jnp.float32).reshape(position.shape + (1,) * (values.ndim - 1)) * frequency
    )
    cosine = jnp.cos(angles)
    sine_part = jnp.sin(angles)
    first_half = values[..., :half_width]
    second_half = values[..., half_width:]
    return jnp.concatenate(
        [
            first_half * cosine - second_half * sine_part,
            second_half * cosine + first_half * sine_part,
        ],
        axis=-1,
    )


def positions(row_ids, block_ids, rows_dev):
    half_width = rows_dev // 2
    device = row_ids // rows_dev
    within = row_ids % rows_dev
    block_num = block_ids.reshape(-1)[device * 2 + within // half_width]
    return block_num * half_width + within % half_width


def body(
    tokens,
    block_ids,
    attn_gain,
    q_weight,
    kv_weight,
    kv_gain,
    uk_weight,
    uv_weight,
    o_weight,
    ffn_gain,
    w_gate,
    w_up,
    w_down,
    routes,
    gate_weights,
):
    tp_count = lax.axis_size("tp")
    seq_count = lax.axis_size("seq")
    tp_index = lax.axis_index("tp")
    seq_index = lax.axis_index("seq")
    sub_rows = tokens.shape[0]
    dev_rows = sub_rows * tp_count
    model_dim = tokens.shape[1]
    head_count = uk_weight.shape[0]
    latent_dim = uk_weight.shape[1]
    nope_dim = uk_weight.shape[2]
    rope_dim = kv_weight.shape[1] - latent_dim
    value_dim = uv_weight.shape[2]
    top_count = routes.shape[1]
    capacity = min(sub_rows, max(2, 3 * sub_rows * top_count // (2 * seq_count)))
    score_scale = (nope_dim + rope_dim) ** (-0.5)
    all_tokens = lax.all_gather(tokens, "tp", axis=0, tiled=True)
    normed = normalize(all_tokens, attn_gain).astype(jnp.bfloat16)
    query_ids = seq_index * dev_rows + jnp.arange(dev_rows, dtype=jnp.int32)
    query_pos = positions(query_ids, block_ids, dev_rows)
    queries = jnp.dot(normed, q_weight, preferred_element_type=jnp.float32).astype(jnp.bfloat16)
    queries = queries.reshape(dev_rows, head_count, nope_dim + rope_dim)
    query_rope = rotate(queries[..., nope_dim:].astype(jnp.float32), query_pos).astype(jnp.bfloat16)
    query_latent = jnp.einsum(
        "thn,hln->thl", queries[..., :nope_dim], uk_weight, preferred_element_type=jnp.float32
    ).astype(jnp.bfloat16)
    projected = jnp.dot(normed, kv_weight, preferred_element_type=jnp.float32)
    latent = normalize(projected[:, :latent_dim], kv_gain).astype(jnp.bfloat16)
    key_rope = rotate(projected[:, latent_dim:], query_pos).astype(jnp.bfloat16)
    latent, key_rope = (latent, key_rope)
    run_max = jnp.full((dev_rows, head_count), -1e30, jnp.float32)
    piece_latent = lax.all_gather(latent, "seq", axis=0, tiled=True)
    piece_rope = lax.all_gather(key_rope, "seq", axis=0, tiled=True)
    count_rows = piece_latent.shape[0]
    key_pos = positions(jnp.arange(count_rows, dtype=jnp.int32), block_ids, dev_rows)
    scores = jnp.einsum(
        "thl,kl->thk", query_latent, piece_latent, preferred_element_type=jnp.float32
    )
    scores = scores + jnp.einsum(
        "thr,kr->thk", query_rope, piece_rope, preferred_element_type=jnp.float32
    )
    scores = scores * score_scale
    allowed = key_pos[None, None, :] <= query_pos[:, None, None]
    scores = jnp.where(allowed, scores, -1e30)
    new_max = jnp.maximum(run_max, jnp.max(scores, axis=-1))
    exp_terms = jnp.where(allowed, jnp.exp(scores - new_max[..., None]), 0.0)
    run_sum = jnp.sum(exp_terms, axis=-1)
    accumulated = jnp.einsum(
        "thk,kl->thl",
        exp_terms.astype(jnp.bfloat16),
        piece_latent,
        preferred_element_type=jnp.float32,
    )
    folded = (new_max, run_sum, accumulated)
    run_max, run_sum, accumulated = folded
    out_latent = (accumulated / run_sum[..., None]).astype(jnp.bfloat16)
    head_out = jnp.einsum(
        "thl,hlv->thv", out_latent, uv_weight, preferred_element_type=jnp.float32
    ).astype(jnp.bfloat16)
    partial_out = jnp.dot(
        head_out.reshape(dev_rows, head_count * value_dim),
        o_weight,
        preferred_element_type=jnp.float32,
    )
    expert_ids = jnp.arange(seq_count, dtype=jnp.int32)

    def slot_table(route_rows):
        flat_ids = route_rows.reshape(-1)
        onehot = (flat_ids[:, None] == expert_ids[None, :]).astype(jnp.int32)
        rank_table = jnp.cumsum(onehot, axis=0) - onehot
        return flat_ids * capacity + jnp.sum(rank_table * onehot, axis=1)

    own_routes = lax.dynamic_slice_in_dim(routes, tp_index * sub_rows, sub_rows, 0)
    own_weights = lax.dynamic_slice_in_dim(gate_weights, tp_index * sub_rows, sub_rows, 0)
    attn_own = lax.psum_scatter(
        partial_out.astype(jnp.bfloat16), "tp", scatter_dimension=0, tiled=True
    ).astype(jnp.float32)
    mixed_rows = (tokens.astype(jnp.float32) + attn_own).astype(jnp.bfloat16)
    normed_own = normalize(mixed_rows, ffn_gain).astype(jnp.bfloat16)
    target = slot_table(own_routes)
    source = jnp.arange(target.shape[0], dtype=jnp.int32) // top_count
    buffer = (
        jnp.zeros((seq_count * capacity, model_dim), jnp.bfloat16)
        .at[target]
        .set(normed_own[source])
    )
    packed = buffer.reshape(seq_count, capacity, model_dim)
    arrived = lax.all_to_all(packed, "seq", split_axis=0, concat_axis=0, tiled=True)
    piece_data = lax.all_gather(arrived, "tp", axis=0, tiled=True)
    flat_rows = piece_data.reshape(-1, model_dim)
    gate_part = jnp.dot(flat_rows, w_gate[0], preferred_element_type=jnp.float32)
    up_part = jnp.dot(flat_rows, w_up[0], preferred_element_type=jnp.float32)
    hidden = (
        (jax.nn.silu(gate_part) * up_part)
        .astype(jnp.bfloat16)
        .reshape(piece_data.shape[0], capacity, -1)
        .reshape(-1, w_up.shape[2])
    )
    down_local = w_down[0]
    expert_out = lax.psum_scatter(
        jnp.dot(hidden, down_local, preferred_element_type=jnp.float32).astype(jnp.bfloat16),
        "tp",
        scatter_dimension=0,
        tiled=True,
    ).astype(jnp.float32)
    expert_out = expert_out.astype(jnp.bfloat16).reshape(seq_count, capacity, model_dim)
    returned = lax.all_to_all(expert_out, "seq", split_axis=0, concat_axis=0, tiled=True).reshape(
        seq_count * capacity, model_dim
    )
    picked = (
        returned[slot_table(own_routes)].astype(jnp.float32).reshape(sub_rows, top_count, model_dim)
    )
    combined = jnp.sum(picked * own_weights[..., None], axis=1)
    return (mixed_rows.astype(jnp.float32) + combined).astype(jnp.bfloat16)


def solution(mesh):
    return jax.shard_map(
        body,
        mesh=mesh,
        in_specs=(
            P(("seq", "tp"), None),
            P(),
            P(),
            P(None, "tp"),
            P(),
            P(),
            P("tp", None, None),
            P("tp", None, None),
            P("tp", None),
            P(),
            P("seq", None, "tp"),
            P("seq", None, "tp"),
            P("seq", "tp", None),
            P("seq", None),
            P("seq", None),
        ),
        out_specs=P(("seq", "tp"), None),
        check_vma=False,
    )
```

profile of v0, /device:TPU:65, one launch (start us, length us, event | category | flops | bytes accessed | tf_op | source)
XLA Modules:
  0.0 593.9 jit_solution(11519764345075057940)
XLA Ops:
  6.6 13.5 %all_gather.12 = bf16[128,2048]{1,0:T(8,128)(2,1)S(1)} all-gather(bf16[32,2048]{1,0:T(8,128)(2,1)} %param.15), channel_id=1, replica_groups=mesh['seq'=64,'tp'=4] {'tp'}, dimensions={0}, use_global_device_ids=true | all-gather | bytes 655360 | tf_op jit(solution)/shard_map/all_gather | solution.py:77
  20.9 2.5 fusion.53
  23.5 0.8 multiply_convert_fusion
  24.6 1.2 gather_fusion.1
  26.9 1.7 convolution_convert_fusion.3
  28.8 48.9 %gather_fusion = s32[8192]{0:T(1024)S(1)} fusion(s32[128]{0:T(128)S(1)} %reshape.560, s32[8192]{0:T(1024)S(1)} %broadcast_clamp_fusion), kind=kCustom, calls=%fused_computation | custom fusion | bytes 98304 | tf_op jit(solution)/shard_map/gather | solution.py:41
  78.7 84.5 %all-gather.4.cloned.1.call-done = bf16[8192,512]{0,1:T(8,128)(2,1)} async-done(((bf16[128,512]{0,1:T(8,128)(2,1)}), bf16[8192,512]{0,1:T(8,128)(2,1)}) %all-gather.4.cloned.1.call-update) | async-done | bytes 8388624 | tf_op jit(solution)/shard_map/all_gather | solution.py:92
  163.2 10.4 %fusion.5 = f32[128,4,8192]{2,0,1:T(8,128)} fusion(bf16[8192,512]{0,1:T(8,128)(2,1)} %all-gather.4.cloned.1.call-done, bf16[4,512,128]{2,1,0:T(8,128)(2,1)S(1)} %copy-done.6, bf16[128,4,192]{0,2,1:T(8,128)(2,1)S(1)} %bitcast.67), kind=kOutput, calls=%fused_computation.11 | convolution fusion | flops 4362338304 | bytes 25821184 | tf_op jit(solution)/shard_map/thl,kl->thk/dot_general | solution.py:96
  173.7 66.5 %all-gather.6.cloned.1.call-done = bf16[8192,64]{0,1:T(8,128)(2,1)} async-done(((bf16[128,64]{0,1:T(8,128)(2,1)}), bf16[8192,64]{0,1:T(8,128)(2,1)}) %all-gather.6.cloned.1.call-update) | async-done | bytes 1048592 | tf_op jit(solution)/shard_map/all_gather | solution.py:93
  240.2 12.0 %fusion.80 = (f32[128,4]{0,1:T(4,128)S(1)}, f32[128,4,8192]{2,0,1:T(8,128)}) fusion(f32[128,4,8192]{2,0,1:T(8,128)} %fusion.5, bf16[8192,64]{0,1:T(8,128)(2,1)} %all-gather.6.cloned.1.call-done, bf16[128,4,32]{0,2,1:T(8,128)(2,1)S(1)} %get-tuple-element.12, bf16[128,4,32]{0,2,1:T(8,128)(2,1)S(1)} %get-tuple-element.11, ...), kind=kOutput, calls=%fused_computation.141 | convolution fusion | flops 553778688 | bytes 35719168 | tf_op jit(solution)/shard_map/thr,kr->thk/dot_general | solution.py:99
  252.2 9.5 %fusion = f32[128,4]{0,1:T(4,128)S(1)} fusion(f32[128,4,8192]{2,0,1:T(8,128)} %get-tuple-element.18, f32[128,4]{0,1:T(4,128)S(1)} %broadcast_maximum_fusion, pred[128,8192]{1,0:T(8,128)(4,1)S(1)} %broadcast_compare_fusion), kind=kLoop, calls=%fused_computation.7 | loop fusion | flops 12582400 | bytes 17829888 | tf_op jit(solution)/shard_map/reduce_sum | solution.py:107
  261.8 13.1 %fusion.33 = bf16[4,128,128]{1,2,0:T(8,128)(2,1)S(1)} fusion(bf16[4,512,128]{2,1,0:T(8,128)(2,1)} %param.22, bf16[8192,512]{0,1:T(8,128)(2,1)} %all-gather.4.cloned.1.call-done, f32[128,4,8192]{2,0,1:T(8,128)} %get-tuple-element.18, f32[128,4]{0,1:T(4,128)S(1)} %broadcast_maximum_fusion, pred[128,8192]{1,0:T(8,128)(4,1)S(1)} %broadcast_compare_fusion, ...), kind=kOutput, calls=%fused_computation.34 | convolution fusion | flops 4375248896 | bytes 26873856 | tf_op jit(solution)/shard_map/thl,hlv->thv/dot_general | solution.py:117
  274.9 1.3 convolution_convert_fusion.1
  276.3 0.8 reduce-window.6
  277.7 19.5 %reduce-scatter.3.cloned.1.call-done = bf16[32,2048]{1,0:T(8,128)(2,1)} async-done(((bf16[128,2048]{1,0:T(8,128)(2,1)}), bf16[32,2048]{1,0:T(8,128)(2,1)}) %reduce-scatter.3.cloned.1.call-update) | async-done | bytes 131088 | tf_op jit(solution)/shard_map/reduce_scatter | solution.py:135
  297.2 1.1 fusion.49
  298.3 1.0 fusion.51
  299.3 4.5 scatter_custom_fusion
  304.3 43.3 %all_to_all.10 = bf16[64,4,2048]{2,1,0:T(4,128)(2,1)} all-to-all(bf16[64,4,2048]{2,1,0:T(4,128)(2,1)S(1)} %reshape.565), channel_id=1, replica_groups=mesh['seq'=64,'tp'=4] {'seq'}, dimensions={0} | all-to-all | bytes 2097152 | tf_op jit(solution)/shard_map/all_to_all | solution.py:148
  347.7 80.0 %all-gather.8.cloned.1.call-done = bf16[256,4,2048]{2,1,0:T(4,128)(2,1)} async-done(((bf16[64,4,2048]{2,1,0:T(4,128)(2,1)}), bf16[256,4,2048]{2,1,0:T(4,128)(2,1)}) %all-gather.8.cloned.1.call-update) | async-done | bytes 4194320 | tf_op jit(solution)/shard_map/all_gather | solution.py:149
  427.7 6.9 %reshape.566 = bf16[1024,2048]{1,0:T(8,128)(2,1)} reshape(bf16[256,4,2048]{2,1,0:T(4,128)(2,1)} %all-gather.8.cloned.1.call-done) | data formatting | bytes 8388608 | tf_op jit(solution)/shard_map/reshape | solution.py:150
  434.6 5.2 fusion.12
  439.8 9.0 %convolution_convert_fusion = bf16[1024,2048]{1,0:T(8,128)(2,1)} fusion(bf16[1,352,2048]{2,1,0:T(8,128)(2,1)S(1)} %copy-done.14, bf16[1024,2048]{1,0:T(8,128)(2,1)} %reshape.566, bf16[1,2048,352]{1,2,0:T(8,128)(2,1)} %param.26, f32[1024,352]{0,1:T(8,128)} %fusion.12), kind=kOutput, calls=%fused_computation.16 | convolution fusion | flops 2957049856 | bytes 12713984 | tf_op jit(solution)/shard_map/dot_general | solution.py:161
  448.8 82.9 %reduce-scatter.5.cloned.1.call-done = bf16[256,2048]{1,0:T(8,128)(2,1)} async-done(((bf16[1024,2048]{1,0:T(8,128)(2,1)}), bf16[256,2048]{1,0:T(8,128)(2,1)}) %reduce-scatter.5.cloned.1.call-update) | async-done | bytes 1048592 | tf_op jit(solution)/shard_map/reduce_scatter | solution.py:160
  531.7 2.3 reshape.567
  534.0 10.3 %all-to-all-start.1 = ((bf16[64,4,2048]{2,1,0:T(4,128)(2,1)}), bf16[64,4,2048]{2,1,0:T(4,128)(2,1)S(1)}, u32[]{:S(2)}, u32[]{:S(2)}) async-start(bf16[64,4,2048]{2,1,0:T(4,128)(2,1)} %reshape.567), calls=%async_computation.3 | async-start | bytes 2097152 | tf_op jit(solution)/shard_map/all_to_all | solution.py:167
  544.5 31.8 %all-to-all-done.1 = bf16[64,4,2048]{2,1,0:T(4,128)(2,1)S(1)} async-done(((bf16[64,4,2048]{2,1,0:T(4,128)(2,1)}), bf16[64,4,2048]{2,1,0:T(4,128)(2,1)S(1)}, u32[]{:S(2)}, u32[]{:S(2)}) %all-to-all-start.1) | async-done | bytes 1048608 | tf_op jit(solution)/shard_map/all_to_all | solution.py:167
  576.3 1.1 reshape.568
  577.4 4.3 gather_fusion.2
  581.8 2.5 reshape.570
  584.3 2.3 multiply_reduce_fusion
  586.7 0.7 fusion.52
  (80 shorter events, 4.8 us)
Async XLA Ops:
  6.5 20.4 %copy-start = (bf16[2048,768]{1,0:T(8,128)(2,1)S(1)}, bf16[2048,768]{1,0:T(8,128)(2,1)}, u32[]{:S(2)}) copy-start(bf16[2048,768]{1,0:T(8,128)(2,1)} %param.18) | copy-start | bytes 9437188
  6.5 20.4 %copy-start.7 = (f32[2048]{0:T(1024)S(1)}, f32[2048]{0:T(1024)}, u32[]{:S(2)}) copy-start(f32[2048]{0:T(1024)} %param.17) | copy-start | bytes 24580
  6.5 16.9 %copy-start.11 = (f32[512]{0:T(512)S(1)}, f32[512]{0:T(512)}, u32[]{:S(2)}) copy-start(f32[512]{0:T(512)} %param.20) | copy-start | bytes 6148
  6.5 17.8 %copy-start.12 = (s32[64,2]{0,1:T(2,128)S(1)}, s32[64,2]{0,1:T(2,128)}, u32[]{:S(2)}) copy-start(s32[64,2]{0,1:T(2,128)} %param.16) | copy-start | bytes 1540
  6.5 156.7 %all-gather.4.cloned.1.call-start = ((), (), s32[]{:S(2)}) async-start(), calls=%async_computation.4 | async-start | bytes 8519680 | tf_op jit(solution)/shard_map/all_gather | solution.py:92
  20.1 0.8 copy-start.2
  24.3 215.9 %all-gather.6.cloned.1.call-start = ((), (), s32[]{:S(2)}) async-start(), calls=%async_computation.5 | async-start | bytes 1064960 | tf_op jit(solution)/shard_map/all_gather | solution.py:93
  26.7 270.5 %reduce-scatter.3.cloned.1.call-start = ((), (), s32[]{:S(2)}) async-start(), calls=%async_computation.6 | async-start | bytes 655360 | tf_op jit(solution)/shard_map/reduce_scatter | solution.py:135
  28.8 49.6 %copy-start.9 = (s32[128,6]{0,1:T(8,128)S(1)}, s32[128,6]{0,1:T(8,128)}, u32[]{:S(2)}) copy-start(s32[128,6]{0,1:T(8,128)} %param.28) | copy-start | bytes 9220
  28.8 134.4 %copy-start.6 = (bf16[4,512,128]{2,1,0:T(8,128)(2,1)S(1)}, bf16[4,512,128]{2,1,0:T(8,128)(2,1)}, u32[]{:S(2)}) copy-start(bf16[4,512,128]{2,1,0:T(8,128)(2,1)} %param.21) | copy-start | bytes 1572868
  261.8 13.1 %copy-start.4 = (bf16[512,2048]{1,0:T(8,128)(2,1)S(1)}, bf16[512,2048]{1,0:T(8,128)(2,1)}, u32[]{:S(2)}) copy-start(bf16[512,2048]{1,0:T(8,128)(2,1)} %param.23) | copy-start | bytes 6291460
  261.8 35.4 %copy-start.3 = (bf16[32,2048]{1,0:T(8,128)(2,1)S(1)}, bf16[32,2048]{1,0:T(8,128)(2,1)}, u32[]{:S(2)}) copy-start(bf16[32,2048]{1,0:T(8,128)(2,1)} %param.15) | copy-start | bytes 393220
  261.8 36.5 %copy-start.8 = (f32[2048]{0:T(1024)S(1)}, f32[2048]{0:T(1024)}, u32[]{:S(2)}) copy-start(f32[2048]{0:T(1024)} %param.24) | copy-start | bytes 24580
  276.2 151.5 %all-gather.8.cloned.1.call-start = ((), (), s32[]{:S(2)}) async-start(), calls=%async_computation.7 | async-start | bytes 5242880 | tf_op jit(solution)/shard_map/all_gather | solution.py:149
  347.6 87.0 %copy-start.13 = (bf16[1,2048,352]{1,2,0:T(8,128)(2,1)S(1)}, bf16[1,2048,352]{1,2,0:T(8,128)(2,1)}, u32[]{:S(2)}) copy-start(bf16[1,2048,352]{1,2,0:T(8,128)(2,1)} %param.25) | copy-start | bytes 4325380
  347.6 184.1 %reduce-scatter.5.cloned.1.call-start = ((), (), s32[]{:S(2)}) async-start(), calls=%async_computation.8 | async-start | bytes 5242880 | tf_op jit(solution)/shard_map/reduce_scatter | solution.py:160
  434.6 5.2 copy-start.14
  448.8 95.5 %copy-start.10 = (f32[128,6]{0,1:T(8,128)S(1)}, f32[128,6]{0,1:T(8,128)}, u32[]{:S(2)}) copy-start(f32[128,6]{0,1:T(8,128)} %param.29) | copy-start | bytes 9220
  534.0 42.3 %all-to-all-start.1 = ((bf16[64,4,2048]{2,1,0:T(4,128)(2,1)}), bf16[64,4,2048]{2,1,0:T(4,128)(2,1)S(1)}, u32[]{:S(2)}, u32[]{:S(2)}) async-start(bf16[64,4,2048]{2,1,0:T(4,128)(2,1)} %reshape.567), calls=%async_computation.3 | async-start | bytes 2097152 | tf_op jit(solution)/shard_map/all_to_all | solution.py:167
  577.4 9.9 %copy-start.1 = (bf16[2048,768]{1,0:T(8,128)(2,1)S(1)}, bf16[2048,768]{1,0:T(8,128)(2,1)}, u32[]{:S(2)}) copy-start(bf16[2048,768]{1,0:T(8,128)(2,1)} %param.18) | copy-start | bytes 9437188
  581.8 4.9 copy-start.5
Sparse Core Ops, SparseCore 0:
  24.4 138.7 all-gather.3
  166.5 73.6 all-gather.5
  276.3 20.8 reduce-scatter.2
  347.7 79.9 all-gather.7
  449.0 82.7 reduce-scatter.4
where the time goes:
time: 594 us
  waiting for transfers between devices  365 us (61%)
  local copies, waits for them, and re-layouts  74 us (12%)
  blocking collectives  56.8 us (10%)
  matrix products  55.2 us (9%)
  other arithmetic  18.5 us (3%)
  between operations  13.5 us (2%)
  starting transfers between devices  10.5 us (2%)
    all_gather x1, waiting for transfers between devices, body(): piece_latent = lax.all_gather(latent, 'seq', axis=0, tiled=True)  84.5 us
    reduce_scatter x1, waiting for transfers between devices, body(): lax.psum_scatter(jnp.dot(hidden, down_local, preferred_element_type=jnp.f...  82.9 us
    all_gather x1, waiting for transfers between devices, body(): piece_data = lax.all_gather(arrived, 'tp', axis=0, tiled=True)  80 us
    all_gather x1, waiting for transfers between devices, body(): piece_rope = lax.all_gather(key_rope, 'seq', axis=0, tiled=True)  66.5 us
    gather x2, local copies, waits for them, and re-layouts, positions(): block_num = block_ids.reshape(-1)[device * 2 + within // half_width]  50.1 us
    all_to_all x1, blocking collectives, body(): lax.all_to_all(packed, 'seq', split_axis=0, concat_axis=0, tiled=True)  43.3 us
    all_to_all x1, waiting for transfers between devices, body(): lax.all_to_all(expert_out, 'seq', split_axis=0, concat_axis=0, tiled=True)  31.8 us
    reduce_scatter x1, waiting for transfers between devices, body(): lax.psum_scatter(partial_out.astype(jnp.bfloat16), 'tp', scatter_dimensio...  19.5 us
  transfers between devices with their start and end apart: 6, of which 6 were waited for; matrix products, arithmetic and copies ran while one was open for 11% of the time, Pallas kernels for 0%

commit v1 on v0

--- a/solution.py
+++ b/solution.py
@@ -89,8 +89,11 @@
     key_rope = rotate(projected[:, latent_dim:], query_pos).astype(jnp.bfloat16)
     latent, key_rope = (latent, key_rope)
     run_max = jnp.full((dev_rows, head_count), -1e30, jnp.float32)
-    piece_latent = lax.all_gather(latent, "seq", axis=0, tiled=True)
-    piece_rope = lax.all_gather(key_rope, "seq", axis=0, tiled=True)
+    piece_latent, piece_rope = jnp.split(
+        lax.all_gather(jnp.concatenate([latent, key_rope], axis=1), "seq", axis=0, tiled=True),
+        [latent.shape[1]],
+        axis=1,
+    )
     count_rows = piece_latent.shape[0]
     key_pos = positions(jnp.arange(count_rows, dtype=jnp.int32), block_ids, dev_rows)
     scores = jnp.einsum(

time: 594 us -> 540 us (0.909)
  waiting for transfers between devices: 365 us -> 310 us
    all_gather x2 -> x1, waiting for transfers between devices: 151 us -> 96 us  [body(): lax.all_gather(jnp.concatenate([latent, key_rope], axis=1), 'seq', axis=0...]
  transfers between devices with their start and end apart: 6 -> 5, of which waited for: 6 -> 5; matrix products, arithmetic and copies ran while one was open for 11% -> 10% of each run, Pallas kernels for 0% -> 0%
where the time goes in v1:
time: 540 us; the launch traced here: 539 us
  waiting for transfers between devices  310 us (57%)
  local copies, waits for them, and re-layouts  74.9 us (14%)
  blocking collectives  56.8 us (11%)
  matrix products  55.4 us (10%)
  other arithmetic  17.9 us (3%)
  between operations  13.5 us (2%)
  starting transfers between devices  10.5 us (2%)
    all_gather x1, waiting for transfers between devices, body(): lax.all_gather(jnp.concatenate([latent, key_rope], axis=1), 'seq', axis=0...  96 us
    reduce_scatter x1, waiting for transfers between devices, body(): lax.psum_scatter(jnp.dot(hidden, down_local, preferred_element_type=jnp.f...  82.9 us
    all_gather x1, waiting for transfers between devices, body(): piece_data = lax.all_gather(arrived, 'tp', axis=0, tiled=True)  80.1 us
    gather x2, local copies, waits for them, and re-layouts, positions(): block_num = block_ids.reshape(-1)[device * 2 + within // half_width]  50.1 us
    all_to_all x1, blocking collectives, body(): lax.all_to_all(packed, 'seq', split_axis=0, concat_axis=0, tiled=True)  43.4 us
    all_to_all x1, waiting for transfers between devices, body(): lax.all_to_all(expert_out, 'seq', split_axis=0, concat_axis=0, tiled=True)  31.8 us
    reduce_scatter x1, waiting for transfers between devices, body(): lax.psum_scatter(partial_out.astype(jnp.bfloat16), 'tp', scatter_dimensio...  19.6 us
    all_gather x1, blocking collectives, body(): all_tokens = lax.all_gather(tokens, 'tp', axis=0, tiled=True)  13.5 us
  transfers between devices with their start and end apart: 5, of which 5 were waited for; matrix products, arithmetic and copies ran while one was open for 10% of the time, Pallas kernels for 0%

profile of v1, /device:TPU:65, one launch (start us, length us, event | category | flops | bytes accessed | tf_op | source)
XLA Modules:
  0.0 539.4 jit_solution(9551517479456234341)
XLA Ops:
  6.6 13.5 %all_gather.9 = bf16[128,2048]{1,0:T(8,128)(2,1)S(1)} all-gather(bf16[32,2048]{1,0:T(8,128)(2,1)} %param.15), channel_id=1, replica_groups=mesh['seq'=64,'tp'=4] {'tp'}, dimensions={0}, use_global_device_ids=true | all-gather | bytes 655360 | tf_op jit(solution)/shard_map/all_gather | solution.py:77
  20.0 0.8 copy-done.2
  21.1 0.8 copy.30
  22.0 1.2 gather_fusion.1
  23.2 2.7 fusion.42
  27.1 1.7 convolution_convert_fusion.3
  29.2 48.9 %gather_fusion = s32[8192]{0:T(1024)S(1)} fusion(s32[128]{0:T(128)S(1)} %reshape.560, s32[8192]{0:T(1024)S(1)} %broadcast_clamp_fusion), kind=kCustom, calls=%fused_computation | custom fusion | bytes 98304 | tf_op jit(solution)/shard_map/gather | solution.py:41
  79.0 96.0 %all-gather.3.cloned.1.call-done = bf16[8192,576]{0,1:T(8,128)(2,1)} async-done(((bf16[128,576]{0,1:T(8,128)(2,1)}), bf16[8192,576]{0,1:T(8,128)(2,1)}) %all-gather.3.cloned.1.call-update) | async-done | bytes 9437200 | tf_op jit(solution)/shard_map/all_gather | solution.py:93
  175.0 10.5 %fusion.7 = f32[128,4,8192]{2,0,1:T(8,128)} fusion(bf16[8192,576]{0,1:T(8,128)(2,1)} %all-gather.3.cloned.1.call-done, bf16[4,512,128]{2,1,0:T(8,128)(2,1)S(1)} %copy-done.6, bf16[128,4,192]{0,2,1:T(8,128)(2,1)S(1)} %bitcast.66), kind=kOutput, calls=%fused_computation.14 | convolution fusion | flops 4362338304 | bytes 25821184 | tf_op jit(solution)/shard_map/thl,kl->thk/dot_general | solution.py:99
  185.5 12.0 %fusion.69 = (f32[128,4]{0,1:T(4,128)S(1)}, f32[128,4,8192]{2,0,1:T(8,128)}) fusion(f32[128,4,8192]{2,0,1:T(8,128)} %fusion.7, bf16[8192,576]{0,1:T(8,128)(2,1)} %all-gather.3.cloned.1.call-done, bf16[128,4,32]{0,2,1:T(8,128)(2,1)S(1)} %get-tuple-element.12, bf16[128,4,32]{0,2,1:T(8,128)(2,1)S(1)} %get-tuple-element.11, ...), kind=kOutput, calls=%fused_computation.140 | convolution fusion | flops 553778688 | bytes 35719168 | tf_op jit(solution)/shard_map/thr,kr->thk/dot_general | solution.py:102
  197.5 9.5 %fusion = f32[128,4]{0,1:T(4,128)S(1)} fusion(f32[128,4,8192]{2,0,1:T(8,128)} %get-tuple-element.18, f32[128,4]{0,1:T(4,128)S(1)} %broadcast_maximum_fusion, pred[128,8192]{1,0:T(8,128)(4,1)S(1)} %broadcast_compare_fusion), kind=kLoop, calls=%fused_computation.7 | loop fusion | flops 12582400 | bytes 17829888 | tf_op jit(solution)/shard_map/reduce_sum | solution.py:110
  207.1 13.1 %fusion.25 = bf16[4,128,128]{1,2,0:T(8,128)(2,1)S(1)} fusion(bf16[4,512,128]{2,1,0:T(8,128)(2,1)} %param.22, bf16[8192,576]{0,1:T(8,128)(2,1)} %all-gather.3.cloned.1.call-done, f32[128,4,8192]{2,0,1:T(8,128)} %get-tuple-element.18, f32[128,4]{0,1:T(4,128)S(1)} %broadcast_maximum_fusion, pred[128,8192]{1,0:T(8,128)(4,1)S(1)} %broadcast_compare_fusion, ...), kind=kOutput, calls=%fused_computation.33 | convolution fusion | flops 4375248896 | bytes 26873856 | tf_op jit(solution)/shard_map/thl,hlv->thv/dot_general | solution.py:120
  220.2 1.3 convolution_convert_fusion.1
  221.5 0.8 reduce-window.6
  223.0 19.6 %reduce-scatter.3.cloned.1.call-done = bf16[32,2048]{1,0:T(8,128)(2,1)} async-done(((bf16[128,2048]{1,0:T(8,128)(2,1)}), bf16[32,2048]{1,0:T(8,128)(2,1)}) %reduce-scatter.3.cloned.1.call-update) | async-done | bytes 131088 | tf_op jit(solution)/shard_map/reduce_scatter | solution.py:138
  242.6 1.1 fusion.38
  243.7 1.0 fusion.40
  244.7 4.5 scatter_custom_fusion
  249.7 43.4 %all_to_all.10 = bf16[64,4,2048]{2,1,0:T(4,128)(2,1)} all-to-all(bf16[64,4,2048]{2,1,0:T(4,128)(2,1)S(1)} %reshape.565), channel_id=1, replica_groups=mesh['seq'=64,'tp'=4] {'seq'}, dimensions={0} | all-to-all | bytes 2097152 | tf_op jit(solution)/shard_map/all_to_all | solution.py:151
  293.1 80.1 %all-gather.5.cloned.1.call-done = bf16[256,4,2048]{2,1,0:T(4,128)(2,1)} async-done(((bf16[64,4,2048]{2,1,0:T(4,128)(2,1)}), bf16[256,4,2048]{2,1,0:T(4,128)(2,1)}) %all-gather.5.cloned.1.call-update) | async-done | bytes 4194320 | tf_op jit(solution)/shard_map/all_gather | solution.py:152
  373.2 6.9 %reshape.566 = bf16[1024,2048]{1,0:T(8,128)(2,1)} reshape(bf16[256,4,2048]{2,1,0:T(4,128)(2,1)} %all-gather.5.cloned.1.call-done) | data formatting | bytes 8388608 | tf_op jit(solution)/shard_map/reshape | solution.py:153
  380.1 5.2 fusion.10
  385.3 9.0 %convolution_convert_fusion = bf16[1024,2048]{1,0:T(8,128)(2,1)} fusion(bf16[1,352,2048]{2,1,0:T(8,128)(2,1)S(1)} %copy-done.13, bf16[1024,2048]{1,0:T(8,128)(2,1)} %reshape.566, bf16[1,2048,352]{1,2,0:T(8,128)(2,1)} %param.26, f32[1024,352]{0,1:T(8,128)} %fusion.10), kind=kOutput, calls=%fused_computation.15 | convolution fusion | flops 2957049856 | bytes 12713984 | tf_op jit(solution)/shard_map/dot_general | solution.py:164
  394.3 82.9 %reduce-scatter.5.cloned.1.call-done = bf16[256,2048]{1,0:T(8,128)(2,1)} async-done(((bf16[1024,2048]{1,0:T(8,128)(2,1)}), bf16[256,2048]{1,0:T(8,128)(2,1)}) %reduce-scatter.5.cloned.1.call-update) | async-done | bytes 1048592 | tf_op jit(solution)/shard_map/reduce_scatter | solution.py:163
  477.2 2.3 reshape.567
  479.5 10.4 %all-to-all-start.1 = ((bf16[64,4,2048]{2,1,0:T(4,128)(2,1)}), bf16[64,4,2048]{2,1,0:T(4,128)(2,1)S(1)}, u32[]{:S(2)}, u32[]{:S(2)}) async-start(bf16[64,4,2048]{2,1,0:T(4,128)(2,1)} %reshape.567), calls=%async_computation.3 | async-start | bytes 2097152 | tf_op jit(solution)/shard_map/all_to_all | solution.py:170
  490.0 31.8 %all-to-all-done.1 = bf16[64,4,2048]{2,1,0:T(4,128)(2,1)S(1)} async-done(((bf16[64,4,2048]{2,1,0:T(4,128)(2,1)}), bf16[64,4,2048]{2,1,0:T(4,128)(2,1)S(1)}, u32[]{:S(2)}, u32[]{:S(2)}) %all-to-all-start.1) | async-done | bytes 1048608 | tf_op jit(solution)/shard_map/all_to_all | solution.py:170
  521.8 1.1 reshape.568
  523.0 4.3 gather_fusion.2
  527.3 2.5 reshape.570
  529.8 2.3 multiply_reduce_fusion
  532.2 0.7 fusion.41
  (75 shorter events, 4.2 us)
Async XLA Ops:
  6.5 20.6 %copy-start = (bf16[2048,768]{1,0:T(8,128)(2,1)S(1)}, bf16[2048,768]{1,0:T(8,128)(2,1)}, u32[]{:S(2)}) copy-start(bf16[2048,768]{1,0:T(8,128)(2,1)} %param.18) | copy-start | bytes 9437188
  6.5 20.6 %copy-start.7 = (f32[2048]{0:T(1024)S(1)}, f32[2048]{0:T(1024)}, u32[]{:S(2)}) copy-start(f32[2048]{0:T(1024)} %param.17) | copy-start | bytes 24580
  6.5 19.7 %copy-start.11 = (f32[512]{0:T(512)S(1)}, f32[512]{0:T(512)}, u32[]{:S(2)}) copy-start(f32[512]{0:T(512)} %param.20) | copy-start | bytes 6148
  6.5 168.5 %all-gather.3.cloned.1.call-start = ((), (), s32[]{:S(2)}) async-start(), calls=%async_computation.4 | async-start | bytes 9584640 | tf_op jit(solution)/shard_map/all_gather | solution.py:93
  20.0 0.8 copy-start.2
  27.0 215.6 %reduce-scatter.3.cloned.1.call-start = ((), (), s32[]{:S(2)}) async-start(), calls=%async_computation.5 | async-start | bytes 655360 | tf_op jit(solution)/shard_map/reduce_scatter | solution.py:138
  29.1 48.9 %copy-start.9 = (s32[128,6]{0,1:T(8,128)S(1)}, s32[128,6]{0,1:T(8,128)}, u32[]{:S(2)}) copy-start(s32[128,6]{0,1:T(8,128)} %param.28) | copy-start | bytes 9220
  29.2 145.9 %copy-start.6 = (bf16[4,512,128]{2,1,0:T(8,128)(2,1)S(1)}, bf16[4,512,128]{2,1,0:T(8,128)(2,1)}, u32[]{:S(2)}) copy-start(bf16[4,512,128]{2,1,0:T(8,128)(2,1)} %param.21) | copy-start | bytes 1572868
  207.0 13.1 %copy-start.4 = (bf16[512,2048]{1,0:T(8,128)(2,1)S(1)}, bf16[512,2048]{1,0:T(8,128)(2,1)}, u32[]{:S(2)}) copy-start(bf16[512,2048]{1,0:T(8,128)(2,1)} %param.23) | copy-start | bytes 6291460
  207.0 35.6 %copy-start.3 = (bf16[32,2048]{1,0:T(8,128)(2,1)S(1)}, bf16[32,2048]{1,0:T(8,128)(2,1)}, u32[]{:S(2)}) copy-start(bf16[32,2048]{1,0:T(8,128)(2,1)} %param.15) | copy-start | bytes 393220
  207.1 36.6 %copy-start.8 = (f32[2048]{0:T(1024)S(1)}, f32[2048]{0:T(1024)}, u32[]{:S(2)}) copy-start(f32[2048]{0:T(1024)} %param.24) | copy-start | bytes 24580
  221.4 151.8 %all-gather.5.cloned.1.call-start = ((), (), s32[]{:S(2)}) async-start(), calls=%async_computation.6 | async-start | bytes 5242880 | tf_op jit(solution)/shard_map/all_gather | solution.py:152
  293.0 87.1 %copy-start.12 = (bf16[1,2048,352]{1,2,0:T(8,128)(2,1)S(1)}, bf16[1,2048,352]{1,2,0:T(8,128)(2,1)}, u32[]{:S(2)}) copy-start(bf16[1,2048,352]{1,2,0:T(8,128)(2,1)} %param.25) | copy-start | bytes 4325380
  293.1 184.2 %reduce-scatter.5.cloned.1.call-start = ((), (), s32[]{:S(2)}) async-start(), calls=%async_computation.7 | async-start | bytes 5242880 | tf_op jit(solution)/shard_map/reduce_scatter | solution.py:163
  380.1 5.2 copy-start.13
  394.3 95.6 %copy-start.10 = (f32[128,6]{0,1:T(8,128)S(1)}, f32[128,6]{0,1:T(8,128)}, u32[]{:S(2)}) copy-start(f32[128,6]{0,1:T(8,128)} %param.29) | copy-start | bytes 9220
  479.5 42.4 %all-to-all-start.1 = ((bf16[64,4,2048]{2,1,0:T(4,128)(2,1)}), bf16[64,4,2048]{2,1,0:T(4,128)(2,1)S(1)}, u32[]{:S(2)}, u32[]{:S(2)}) async-start(bf16[64,4,2048]{2,1,0:T(4,128)(2,1)} %reshape.567), calls=%async_computation.3 | async-start | bytes 2097152 | tf_op jit(solution)/shard_map/all_to_all | solution.py:170
  523.0 9.9 %copy-start.1 = (bf16[2048,768]{1,0:T(8,128)(2,1)S(1)}, bf16[2048,768]{1,0:T(8,128)(2,1)}, u32[]{:S(2)}) copy-start(bf16[2048,768]{1,0:T(8,128)(2,1)} %param.18) | copy-start | bytes 9437188
  527.3 4.9 copy-start.5
Sparse Core Ops, SparseCore 0:
  27.2 147.8 all-gather.2
  221.6 20.9 reduce-scatter.2
  293.2 80.0 all-gather.4
  394.4 82.7 reduce-scatter.4
